TPU v7x, 32 devices: a whole 2x2x4 slice. The times are simulated.
32 devices in a mesh: gz: 8 (over z, x), gy: 4 (over y, core).
Axes of the slice: x: 2, y: 2, z: 4, core: 2. Of those that a mesh axis runs over, the one named last changes fastest.
Arguments:
- features: bfloat16 [8, 4, 1, 64, 512], P('gz', 'gy'), may hold values from -6 to 6
- cotangent: bfloat16 [8, 4, 1, 64, 512], P('gz', 'gy'), may hold values from -6 to 6
- first_weight: bfloat16 [64, 1728], replicated, may hold values from -0.15625 to 0.15625
- second_weight: bfloat16 [64, 1728], replicated, may hold values from -0.15625 to 0.15625
- positions: int32 [8, 4, 1], P('gz', 'gy'), may hold values from 0 to 3, as said below
- counts: int32 [8, 4], P('gz', 'gy'), may hold values from 1 to 1, as said below
Outputs:
- output: bfloat16 [8, 4, 1, 64, 512], P('gz', 'gy')
- input_grad: bfloat16 [8, 4, 1, 64, 512], P('gz', 'gy')
- first_grad: float32 [64, 1728], replicated
- second_grad: float32 [64, 1728], replicated
Inputs may be any that keep to these rules, and one draw needn't show every extreme that they name: The first counts[i, j] positions of each device are distinct. `counts`: some device has all 1 slots active.
All inputs are finite; a program needn't handle non-finite values.
Results may differ from a plain program's by a relative error of at most 0.0052.
Values may be sent and summed in bfloat16 or wider, within the bound.
A program may use at most 64 MiB of HBM per device.

v0:
```python
import math

import jax
import jax.numpy as jnp
from jax import lax
from jax.sharding import PartitionSpec as P

E = 8
BY = 2
BX = 2


def padded_2(cells, sides, width):
    for axis, dim in sides:
        count = lax.axis_size(axis)
        ends = count - 1
        head = lax.slice_in_dim(cells, 0, width, axis=dim)
        tail = lax.slice_in_dim(cells, cells.shape[dim] - width, cells.shape[dim], axis=dim)
        cells = jnp.concatenate(
            [
                lax.ppermute(tail, axis, [(i, (i + 1) % count) for i in range(ends)]),
                cells,
                lax.ppermute(head, axis, [((i + 1) % count, i) for i in range(ends)]),
            ],
            axis=dim,
        )
    return cells


def silu_slope(value):
    sig = jax.nn.sigmoid(value)
    return sig * (1.0 + value * (1.0 - sig))


def to_slab(bricks, places, live):
    channels = bricks.shape[1]
    masked = jnp.where(live[:, None, None], bricks, jnp.zeros_like(bricks))
    grid = jnp.zeros((BY * BX, channels, E**3), bricks.dtype).at[places].set(masked)
    grid = grid.reshape(BY, BX, channels, E, E, E)
    return grid.transpose(2, 3, 0, 4, 1, 5).reshape(channels, E, BY * E, BX * E)


def patch_of(padded, place):
    channels = padded.shape[0]
    zero = jnp.zeros((), jnp.int32)
    row_y = place // BX * E
    row_x = place % BX * E
    cube = lax.dynamic_slice(padded, (zero, zero, row_y, row_x), (channels, E + 2, E + 2, E + 2))
    pieces = []
    for depth in range(3):
        for height in range(3):
            for across in range(3):
                pieces.append(
                    cube[:, depth : depth + E, height : height + E, across : across + E].reshape(
                        channels, E**3
                    )
                )
    return jnp.concatenate(pieces, axis=0)


def flip_weight(weight):
    channels = weight.shape[0]
    return (
        weight.reshape(channels, 27, channels)[:, ::-1, :]
        .transpose(2, 1, 0)
        .reshape(channels, 27 * channels)
    )


def extend(bricks, places, live):
    wider = padded_2(to_slab(bricks, places, live), (("gz", 1), ("gy", 2)), 1)
    return jnp.pad(wider, ((0, 0), (0, 0), (0, 0), (1, 1)))


def convolve(padded, weight, places):

    def single(place):
        return jnp.dot(weight, patch_of(padded, place), preferred_element_type=jnp.float32)

    return lax.map(single, places)


def spread_and_terms(grad_pad, other_pad, flipped, grads, places):
    channels = grads.shape[1]

    def step(total, item):
        place, grad_here = item
        spread = jnp.dot(flipped, patch_of(grad_pad, place), preferred_element_type=jnp.float32)
        term = lax.dot_general(
            grad_here,
            patch_of(other_pad, place),
            (((1,), (1,)), ((), ())),
            preferred_element_type=jnp.float32,
        )
        return (total + term, spread)

    return lax.scan(step, jnp.zeros((channels, 27 * channels), jnp.float32), (places, grads))


def body(features, cotangent, first_weight, second_weight, positions, counts):
    bricks = features[0, 0]
    upstream = cotangent[0, 0]
    places = positions[0, 0]
    slots = bricks.shape[0]
    live = lax.iota(jnp.int32, slots) < counts[0, 0]
    live_col = live[:, None, None]
    scale = 1.0 / math.sqrt(lax.axis_size("gz") * lax.axis_size("gy") * slots * E**3)
    input_pad = extend(bricks, places, live)
    first_pre = jnp.where(live_col, convolve(input_pad, first_weight, places), 0.0)
    first_act = jax.nn.silu(first_pre).astype(jnp.bfloat16)
    act_pad = extend(first_act, places, live)
    summed = bricks.astype(jnp.float32) + convolve(act_pad, second_weight, places)
    output = jnp.where(live_col, jax.nn.silu(summed), 0.0).astype(jnp.bfloat16)
    grad_sum = jnp.where(live_col, upstream.astype(jnp.float32) * silu_slope(summed), 0.0).astype(
        jnp.bfloat16
    )
    grad_pad = extend(grad_sum, places, live)
    second_total, act_grad = spread_and_terms(
        grad_pad, act_pad, flip_weight(second_weight), grad_sum, places
    )
    pre_grad = jnp.where(live_col, act_grad * silu_slope(first_pre), 0.0).astype(jnp.bfloat16)
    pre_pad = extend(pre_grad, places, live)
    first_total, input_spread = spread_and_terms(
        pre_pad, input_pad, flip_weight(first_weight), pre_grad, places
    )
    input_grad = jnp.where(live_col, grad_sum.astype(jnp.float32) + input_spread, 0.0).astype(
        jnp.bfloat16
    )
    first_sum, second_sum = lax.psum((first_total, second_total), ("gz", "gy"))
    first_grad = first_sum * scale
    second_grad = second_sum * scale
    return (output[None, None], input_grad[None, None], first_grad, second_grad)


def solution(mesh):
    return jax.shard_map(
        body,
        mesh=mesh,
        in_specs=(
            P("gz", "gy", None, None, None),
            P("gz", "gy", None, None, None),
            P(),
            P(),
            P("gz", "gy", None),
            P("gz", "gy"),
        ),
        out_specs=(P("gz", "gy", None, None, None), P("gz", "gy", None, None, None), P(), P()),
        check_vma=False,
    )
```

profile of v0, /device:TPU:0, one launch (start us, length us, event | category | flops | bytes accessed | tf_op | source)
XLA Modules:
  0.0 266.7 jit_solution(11983859026510268498)
XLA Ops:
  8.5 1.0 copy.10
  9.5 1.4 and_reduce_fusion
  11.7 1.3 collective-permute-start.1
  13.0 5.5 %collective-permute-start = (bf16[64,1,16,16]{0,3,2,1:T(8,128)(2,1)S(1)}, bf16[64,1,16,16]{0,3,2,1:T(8,128)(2,1)S(1)}, u32[]{:S(2)}, u32[]{:S(2)}) collective-permute-start(bf16[64,1,16,16]{0,3,2,1:T(8,128)(2,1)S(1)} %get-tuple-element.151), channel_id=1, source_target_pairs={{0,4},{4,8},{8,12},{12,16},{16,20},{20,24},{24,28},{1,5},{5,9},{9,... | collective-permute-start | bytes 98312 | tf_op jit(solution)/shard_map/ppermute | solution.py:21
  18.8 1.7 collective-permute-done
  20.6 1.3 collective-permute-start.3
  21.9 3.0 %collective-permute-start.2 = (bf16[64,10,1,16]{0,3,2,1:T(8,128)(2,1)S(1)}, bf16[64,10,1,16]{0,3,2,1:T(8,128)(2,1)S(1)}, u32[]{:S(2)}, u32[]{:S(2)}) collective-permute-start(bf16[64,10,1,16]{0,3,2,1:T(8,128)(2,1)S(1)} %get-tuple-element.143), channel_id=1, source_target_pairs={{0,1},{1,2},{2,3},{4,5},{5,6},{6,7},{8,9},{9,10},{10,11},{12,13},{... | collective-permute-start | bytes 61448 | tf_op jit(solution)/shard_map/ppermute | solution.py:21
  25.8 1.1 fusion.16
  27.1 1.4 fusion.62
  28.6 5.0 %concatenate.57 = bf16[1728,512]{0,1:T(8,128)(2,1)S(1)} concatenate(bf16[64,512]{0,1:T(8,128)(2,1)S(1)} %bitcast.217, bf16[64,512]{0,1:T(8,128)(2,1)S(1)} %bitcast.216, bf16[64,512]{0,1:T(8,128)(2,1)S(1)} %bitcast.215, bf16[64,512]{0,1:T(8,128)(2,1)S(1)} %bitcast.214, bf16[64,512]{0,1:T(8,128)(2,1)S(1)} %bitcast.213, bf16[64,512]{0,1:T(8,128)(2,1)S(1)} %bitcast.212, ...), dimensions={0} | concatenate | bytes 3538944 | tf_op jit(solution)/shard_map/while/body/eval_jaxpr/concatenate | solution.py:58
  35.3 1.3 collective-permute-start.5
  36.6 5.3 %collective-permute-start.4 = (bf16[64,1,16,16]{0,3,2,1:T(8,128)(2,1)S(1)}, bf16[64,1,16,16]{0,3,2,1:T(8,128)(2,1)S(1)}, u32[]{:S(2)}, u32[]{:S(2)}) collective-permute-start(bf16[64,1,16,16]{0,3,2,1:T(8,128)(2,1)S(1)} %get-tuple-element.149), channel_id=1, source_target_pairs={{0,4},{4,8},{8,12},{12,16},{16,20},{20,24},{24,28},{1,5},{5,9},{9,... | collective-permute-start | bytes 98312 | tf_op jit(solution)/shard_map/ppermute | solution.py:21
  42.2 2.8 %collective-permute-done.4 = bf16[64,1,16,16]{0,3,2,1:T(8,128)(2,1)S(1)} collective-permute-done((bf16[64,1,16,16]{0,3,2,1:T(8,128)(2,1)S(1)}, bf16[64,1,16,16]{0,3,2,1:T(8,128)(2,1)S(1)}, u32[]{:S(2)}, u32[]{:S(2)}) %collective-permute-start.4) | collective-permute-done | bytes 32800 | tf_op jit(solution)/shard_map/ppermute | solution.py:21
  45.1 1.3 collective-permute-start.7
  46.4 3.0 %collective-permute-start.6 = (bf16[64,10,1,16]{0,3,2,1:T(8,128)(2,1)S(1)}, bf16[64,10,1,16]{0,3,2,1:T(8,128)(2,1)S(1)}, u32[]{:S(2)}, u32[]{:S(2)}) collective-permute-start(bf16[64,10,1,16]{0,3,2,1:T(8,128)(2,1)S(1)} %get-tuple-element.141), channel_id=1, source_target_pairs={{0,1},{1,2},{2,3},{4,5},{5,6},{6,7},{8,9},{9,10},{10,11},{12,13},{... | collective-permute-start | bytes 61448 | tf_op jit(solution)/shard_map/ppermute | solution.py:21
  49.4 0.8 collective-permute-done.6
  51.9 1.6 fusion.60
  53.5 5.6 %concatenate.60 = bf16[1728,512]{0,1:T(8,128)(2,1)} concatenate(bf16[64,512]{0,1:T(8,128)(2,1)} %bitcast.225, bf16[64,512]{0,1:T(8,128)(2,1)S(1)} %bitcast.224, bf16[64,512]{0,1:T(8,128)(2,1)S(1)} %bitcast.223, bf16[64,512]{0,1:T(8,128)(2,1)S(1)} %bitcast.222, bf16[64,512]{0,1:T(8,128)(2,1)S(1)} %bitcast.221, bf16[64,512]{0,1:T(8,128)(2,1)S(1)} %bitcast.220, ...), dimensions={0} | concatenate | bytes 3538944 | tf_op jit(solution)/shard_map/while/body/eval_jaxpr/concatenate | solution.py:58
  59.2 2.2 fusion
  63.1 1.3 collective-permute-start.9
  64.4 5.6 %collective-permute-start.8 = (bf16[64,1,16,16]{0,3,2,1:T(8,128)(2,1)}, bf16[64,1,16,16]{0,3,2,1:T(8,128)(2,1)}, u32[]{:S(2)}, u32[]{:S(2)}) collective-permute-start(bf16[64,1,16,16]{0,3,2,1:T(8,128)(2,1)} %get-tuple-element.147), channel_id=1, source_target_pairs={{0,4},{4,8},{8,12},{12,16},{16,20},{20,24},{24,28},{1,5},{5,9},{9,... | collective-permute-start | bytes 98312 | tf_op jit(solution)/shard_map/ppermute | solution.py:21
  70.0 1.3 reshape.911
  71.8 2.0 rev.7
  73.8 2.9 %copy.19 = bf16[64,27,64]{2,1,0:T(8,128)(2,1)} copy(bf16[64,27,64]{0,1,2:T(8,128)(2,1)} %bitcast.208) | data formatting | bytes 442368 | tf_op jit(solution)/shard_map/transpose | solution.py:65
  76.7 1.4 reshape.912
  78.1 1.2 rev.6
  79.3 2.1 copy.16
  81.5 1.1 reshape.880
  83.3 1.3 collective-permute-start.11
  84.6 5.4 %collective-permute-start.10 = (bf16[64,10,1,16]{0,3,2,1:T(8,128)(2,1)S(1)}, bf16[64,10,1,16]{0,3,2,1:T(8,128)(2,1)S(1)}, u32[]{:S(2)}, u32[]{:S(2)}) collective-permute-start(bf16[64,10,1,16]{0,3,2,1:T(8,128)(2,1)S(1)} %get-tuple-element.139), channel_id=1, source_target_pairs={{0,1},{1,2},{2,3},{4,5},{5,6},{6,7},{8,9},{9,10},{10,11},{12,13},{... | collective-permute-start | bytes 61448 | tf_op jit(solution)/shard_map/ppermute | solution.py:21
  90.0 2.7 %fusion.65 = f32[64,1728]{1,0:T(8,128)} fusion(bf16[64,512]{1,0:T(8,128)(2,1)S(1)} %get-tuple-element.133, bf16[1728,512]{0,1:T(8,128)(2,1)} %concatenate.60), kind=kOutput, calls=%fused_computation.119 | convolution fusion | flops 113246208 | bytes 2277376 | tf_op jit(solution)/shard_map/while/body/eval_jaxpr/dot_general | solution.py:89
  92.7 1.6 fusion.34
  95.1 1.6 fusion.58
  96.7 5.6 %concatenate.63 = bf16[1728,512]{0,1:T(8,128)(2,1)} concatenate(bf16[64,512]{0,1:T(8,128)(2,1)} %bitcast.233, bf16[64,512]{0,1:T(8,128)(2,1)S(1)} %bitcast.232, bf16[64,512]{0,1:T(8,128)(2,1)S(1)} %bitcast.231, bf16[64,512]{0,1:T(8,128)(2,1)S(1)} %bitcast.230, bf16[64,512]{0,1:T(8,128)(2,1)S(1)} %bitcast.229, bf16[64,512]{0,1:T(8,128)(2,1)S(1)} %bitcast.228, ...), dimensions={0} | concatenate | bytes 3538944 | tf_op jit(solution)/shard_map/while/body/eval_jaxpr/concatenate | solution.py:58
  102.3 2.2 fusion.7
  105.5 1.3 collective-permute-start.13
  106.8 5.2 %collective-permute-start.12 = (bf16[64,1,16,16]{0,3,2,1:T(8,128)(2,1)S(1)}, bf16[64,1,16,16]{0,3,2,1:T(8,128)(2,1)S(1)}, u32[]{:S(2)}, u32[]{:S(2)}) collective-permute-start(bf16[64,1,16,16]{0,3,2,1:T(8,128)(2,1)S(1)} %get-tuple-element.145), channel_id=1, source_target_pairs={{0,4},{4,8},{8,12},{12,16},{16,20},{20,24},{24,28},{1,5},{5,9},{9,... | collective-permute-start | bytes 98312 | tf_op jit(solution)/shard_map/ppermute | solution.py:21
  112.7 1.2 collective-permute-done.12
  113.9 1.3 collective-permute-start.15
  115.2 4.3 %collective-permute-start.14 = (bf16[64,10,1,16]{0,3,2,1:T(8,128)(2,1)S(1)}, bf16[64,10,1,16]{0,3,2,1:T(8,128)(2,1)S(1)}, u32[]{:S(2)}, u32[]{:S(2)}) collective-permute-start(bf16[64,10,1,16]{0,3,2,1:T(8,128)(2,1)S(1)} %get-tuple-element.137), channel_id=1, source_target_pairs={{0,1},{1,2},{2,3},{4,5},{5,6},{6,7},{8,9},{9,10},{10,11},{12,13},{... | collective-permute-start | bytes 61448 | tf_op jit(solution)/shard_map/ppermute | solution.py:21
  119.5 1.2 fusion.64
  121.6 1.4 fusion.56
  123.0 1.0 fusion.57
  124.0 4.1 %concatenate.66 = bf16[1728,512]{0,1:T(8,128)(2,1)S(1)} concatenate(bf16[64,512]{0,1:T(8,128)(2,1)} %bitcast.317, bf16[64,512]{0,1:T(8,128)(2,1)} %bitcast.316, bf16[64,512]{0,1:T(8,128)(2,1)} %bitcast.315, bf16[64,512]{0,1:T(8,128)(2,1)} %bitcast.314, bf16[64,512]{0,1:T(8,128)(2,1)} %bitcast.313, bf16[64,512]{0,1:T(8,128)(2,1)} %bitcast.312, bf16[64,512]{0,1:T(8,128)(2,1)} %bitcast.311, ...), dimensions={0} | concatenate | bytes 3538944 | tf_op jit(solution)/shard_map/while/body/eval_jaxpr/concatenate | solution.py:58
  128.1 1.3 fusion.8
  129.4 126.8 %all-reduce.7.cloned.1.call-done = (f32[64,1728]{1,0:T(8,128)}, f32[64,1728]{1,0:T(8,128)}) async-done(((f32[64,1728]{1,0:T(8,128)}, f32[64,1728]{1,0:T(8,128)}), (f32[64,1728]{1,0:T(8,128)}, f32[64,1728]{1,0:T(8,128)})) %all-reduce.7.cloned.1.call-update) | async-done | bytes 884752 | tf_op jit(solution)/shard_map/psum | solution.py:129
  256.2 1.8 broadcast_multiply_fusion.1
  258.0 1.8 broadcast_multiply_fusion
  (63 shorter events, 12.0 us)
Async XLA Ops:
  7.2 249.0 %all-reduce.7.cloned.1.call-start = ((), (), s32[]{:S(2)}) async-start(), calls=%async_computation | async-start | bytes 1835008 | tf_op jit(solution)/shard_map/psum | solution.py:129
  11.7 7.1 %collective-permute-start.1 = (bf16[64,1,16,16]{0,3,2,1:T(8,128)(2,1)S(1)}, bf16[64,1,16,16]{0,3,2,1:T(8,128)(2,1)S(1)}, u32[]{:S(2)}, u32[]{:S(2)}) collective-permute-start(bf16[64,1,16,16]{0,3,2,1:T(8,128)(2,1)S(1)} %get-tuple-element.150), channel_id=1, source_target_pairs={{4,0},{8,4},{12,8},{16,12},{20,16},{24,20},{28,24},{5,1},{9,5},{13... | collective-permute-start | bytes 98312 | tf_op jit(solution)/shard_map/ppermute | solution.py:23
  13.0 7.5 %collective-permute-start = (bf16[64,1,16,16]{0,3,2,1:T(8,128)(2,1)S(1)}, bf16[64,1,16,16]{0,3,2,1:T(8,128)(2,1)S(1)}, u32[]{:S(2)}, u32[]{:S(2)}) collective-permute-start(bf16[64,1,16,16]{0,3,2,1:T(8,128)(2,1)S(1)} %get-tuple-element.151), channel_id=1, source_target_pairs={{0,4},{4,8},{8,12},{12,16},{16,20},{20,24},{24,28},{1,5},{5,9},{9,... | collective-permute-start | bytes 98312 | tf_op jit(solution)/shard_map/ppermute | solution.py:21
  20.6 4.7 %collective-permute-start.3 = (bf16[64,10,1,16]{0,3,2,1:T(8,128)(2,1)S(1)}, bf16[64,10,1,16]{0,3,2,1:T(8,128)(2,1)S(1)}, u32[]{:S(2)}, u32[]{:S(2)}) collective-permute-start(bf16[64,10,1,16]{0,3,2,1:T(8,128)(2,1)S(1)} %get-tuple-element.142), channel_id=1, source_target_pairs={{1,0},{2,1},{3,2},{5,4},{6,5},{7,6},{9,8},{10,9},{11,10},{13,12},{... | collective-permute-start | bytes 61448 | tf_op jit(solution)/shard_map/ppermute | solution.py:23
  21.9 3.9 %collective-permute-start.2 = (bf16[64,10,1,16]{0,3,2,1:T(8,128)(2,1)S(1)}, bf16[64,10,1,16]{0,3,2,1:T(8,128)(2,1)S(1)}, u32[]{:S(2)}, u32[]{:S(2)}) collective-permute-start(bf16[64,10,1,16]{0,3,2,1:T(8,128)(2,1)S(1)} %get-tuple-element.143), channel_id=1, source_target_pairs={{0,1},{1,2},{2,3},{4,5},{5,6},{6,7},{8,9},{9,10},{10,11},{12,13},{... | collective-permute-start | bytes 61448 | tf_op jit(solution)/shard_map/ppermute | solution.py:21
  28.6 5.0 %copy-start = (bf16[64,1728]{1,0:T(8,128)(2,1)S(1)}, bf16[64,1728]{1,0:T(8,128)(2,1)}, u32[]{:S(2)}) copy-start(bf16[64,1728]{1,0:T(8,128)(2,1)} %param.16) | copy-start | bytes 663556
  34.3 16.8 %copy-start.2 = (f32[64,512]{1,0:T(8,128)}, f32[64,512]{1,0:T(8,128)S(1)}, u32[]{:S(2)}) copy-start(f32[64,512]{1,0:T(8,128)S(1)} %fusion.5) | copy-start | bytes 393220
  35.3 6.9 %collective-permute-start.5 = (bf16[64,1,16,16]{0,3,2,1:T(8,128)(2,1)S(1)}, bf16[64,1,16,16]{0,3,2,1:T(8,128)(2,1)S(1)}, u32[]{:S(2)}, u32[]{:S(2)}) collective-permute-start(bf16[64,1,16,16]{0,3,2,1:T(8,128)(2,1)S(1)} %get-tuple-element.148), channel_id=1, source_target_pairs={{4,0},{8,4},{12,8},{16,12},{20,16},{24,20},{28,24},{5,1},{9,5},{13... | collective-permute-start | bytes 98312 | tf_op jit(solution)/shard_map/ppermute | solution.py:23
  36.6 8.4 %collective-permute-start.4 = (bf16[64,1,16,16]{0,3,2,1:T(8,128)(2,1)S(1)}, bf16[64,1,16,16]{0,3,2,1:T(8,128)(2,1)S(1)}, u32[]{:S(2)}, u32[]{:S(2)}) collective-permute-start(bf16[64,1,16,16]{0,3,2,1:T(8,128)(2,1)S(1)} %get-tuple-element.149), channel_id=1, source_target_pairs={{0,4},{4,8},{8,12},{12,16},{16,20},{20,24},{24,28},{1,5},{5,9},{9,... | collective-permute-start | bytes 98312 | tf_op jit(solution)/shard_map/ppermute | solution.py:21
  45.1 4.3 %collective-permute-start.7 = (bf16[64,10,1,16]{0,3,2,1:T(8,128)(2,1)S(1)}, bf16[64,10,1,16]{0,3,2,1:T(8,128)(2,1)S(1)}, u32[]{:S(2)}, u32[]{:S(2)}) collective-permute-start(bf16[64,10,1,16]{0,3,2,1:T(8,128)(2,1)S(1)} %get-tuple-element.140), channel_id=1, source_target_pairs={{1,0},{2,1},{3,2},{5,4},{6,5},{7,6},{9,8},{10,9},{11,10},{13,12},{... | collective-permute-start | bytes 61448 | tf_op jit(solution)/shard_map/ppermute | solution.py:23
  46.4 3.9 %collective-permute-start.6 = (bf16[64,10,1,16]{0,3,2,1:T(8,128)(2,1)S(1)}, bf16[64,10,1,16]{0,3,2,1:T(8,128)(2,1)S(1)}, u32[]{:S(2)}, u32[]{:S(2)}) collective-permute-start(bf16[64,10,1,16]{0,3,2,1:T(8,128)(2,1)S(1)} %get-tuple-element.141), channel_id=1, source_target_pairs={{0,1},{1,2},{2,3},{4,5},{5,6},{6,7},{8,9},{9,10},{10,11},{12,13},{... | collective-permute-start | bytes 61448 | tf_op jit(solution)/shard_map/ppermute | solution.py:21
  51.9 1.6 copy-start.4
  53.5 5.7 %copy-start.1 = (bf16[64,1728]{1,0:T(8,128)(2,1)S(1)}, bf16[64,1728]{1,0:T(8,128)(2,1)}, u32[]{:S(2)}) copy-start(bf16[64,1728]{1,0:T(8,128)(2,1)} %param.17) | copy-start | bytes 663556
  53.5 5.7 %copy-start.5 = (bf16[1,1,1,64,512]{4,3,2,1,0:T(8,128)(2,1)S(1)}, bf16[1,1,1,64,512]{4,3,2,1,0:T(8,128)(2,1)}, u32[]{:S(2)}) copy-start(bf16[1,1,1,64,512]{4,3,2,1,0:T(8,128)(2,1)} %param.14) | copy-start | bytes 196612
  59.2 2.2 copy-start.6
  63.1 19.5 %collective-permute-start.9 = (bf16[64,1,16,16]{0,3,2,1:T(8,128)(2,1)}, bf16[64,1,16,16]{0,3,2,1:T(8,128)(2,1)}, u32[]{:S(2)}, u32[]{:S(2)}) collective-permute-start(bf16[64,1,16,16]{0,3,2,1:T(8,128)(2,1)} %get-tuple-element.146), channel_id=1, source_target_pairs={{4,0},{8,4},{12,8},{16,12},{20,16},{24,20},{28,24},{5,1},{9,5},{13... | collective-permute-start | bytes 98312 | tf_op jit(solution)/shard_map/ppermute | solution.py:23
  64.4 18.2 %collective-permute-start.8 = (bf16[64,1,16,16]{0,3,2,1:T(8,128)(2,1)}, bf16[64,1,16,16]{0,3,2,1:T(8,128)(2,1)}, u32[]{:S(2)}, u32[]{:S(2)}) collective-permute-start(bf16[64,1,16,16]{0,3,2,1:T(8,128)(2,1)} %get-tuple-element.147), channel_id=1, source_target_pairs={{0,4},{4,8},{8,12},{12,16},{16,20},{20,24},{24,28},{1,5},{5,9},{9,... | collective-permute-start | bytes 98312 | tf_op jit(solution)/shard_map/ppermute | solution.py:21
  83.3 9.4 %collective-permute-start.11 = (bf16[64,10,1,16]{0,3,2,1:T(8,128)(2,1)S(1)}, bf16[64,10,1,16]{0,3,2,1:T(8,128)(2,1)S(1)}, u32[]{:S(2)}, u32[]{:S(2)}) collective-permute-start(bf16[64,10,1,16]{0,3,2,1:T(8,128)(2,1)S(1)} %get-tuple-element.138), channel_id=1, source_target_pairs={{1,0},{2,1},{3,2},{5,4},{6,5},{7,6},{9,8},{10,9},{11,10},{13,12},{... | collective-permute-start | bytes 61448 | tf_op jit(solution)/shard_map/ppermute | solution.py:23
  84.6 8.1 %collective-permute-start.10 = (bf16[64,10,1,16]{0,3,2,1:T(8,128)(2,1)S(1)}, bf16[64,10,1,16]{0,3,2,1:T(8,128)(2,1)S(1)}, u32[]{:S(2)}, u32[]{:S(2)}) collective-permute-start(bf16[64,10,1,16]{0,3,2,1:T(8,128)(2,1)S(1)} %get-tuple-element.139), channel_id=1, source_target_pairs={{0,1},{1,2},{2,3},{4,5},{5,6},{6,7},{8,9},{9,10},{10,11},{12,13},{... | collective-permute-start | bytes 61448 | tf_op jit(solution)/shard_map/ppermute | solution.py:21
  96.7 5.6 %copy-start.3 = (f32[64,512]{1,0:T(8,128)S(1)}, f32[64,512]{1,0:T(8,128)}, u32[]{:S(2)}) copy-start(f32[64,512]{1,0:T(8,128)} %copy-done.2) | copy-start | bytes 393220
  105.5 7.2 %collective-permute-start.13 = (bf16[64,1,16,16]{0,3,2,1:T(8,128)(2,1)S(1)}, bf16[64,1,16,16]{0,3,2,1:T(8,128)(2,1)S(1)}, u32[]{:S(2)}, u32[]{:S(2)}) collective-permute-start(bf16[64,1,16,16]{0,3,2,1:T(8,128)(2,1)S(1)} %get-tuple-element.144), channel_id=1, source_target_pairs={{4,0},{8,4},{12,8},{16,12},{20,16},{24,20},{28,24},{5,1},{9,5},{13... | collective-permute-start | bytes 98312 | tf_op jit(solution)/shard_map/ppermute | solution.py:23
  106.8 7.1 %collective-permute-start.12 = (bf16[64,1,16,16]{0,3,2,1:T(8,128)(2,1)S(1)}, bf16[64,1,16,16]{0,3,2,1:T(8,128)(2,1)S(1)}, u32[]{:S(2)}, u32[]{:S(2)}) collective-permute-start(bf16[64,1,16,16]{0,3,2,1:T(8,128)(2,1)S(1)} %get-tuple-element.145), channel_id=1, source_target_pairs={{0,4},{4,8},{8,12},{12,16},{16,20},{20,24},{24,28},{1,5},{5,9},{9,... | collective-permute-start | bytes 98312 | tf_op jit(solution)/shard_map/ppermute | solution.py:21
  113.9 6.8 %collective-permute-start.15 = (bf16[64,10,1,16]{0,3,2,1:T(8,128)(2,1)S(1)}, bf16[64,10,1,16]{0,3,2,1:T(8,128)(2,1)S(1)}, u32[]{:S(2)}, u32[]{:S(2)}) collective-permute-start(bf16[64,10,1,16]{0,3,2,1:T(8,128)(2,1)S(1)} %get-tuple-element.136), channel_id=1, source_target_pairs={{1,0},{2,1},{3,2},{5,4},{6,5},{7,6},{9,8},{10,9},{11,10},{13,12},{... | collective-permute-start | bytes 61448 | tf_op jit(solution)/shard_map/ppermute | solution.py:23
  115.2 5.5 %collective-permute-start.14 = (bf16[64,10,1,16]{0,3,2,1:T(8,128)(2,1)S(1)}, bf16[64,10,1,16]{0,3,2,1:T(8,128)(2,1)S(1)}, u32[]{:S(2)}, u32[]{:S(2)}) collective-permute-start(bf16[64,10,1,16]{0,3,2,1:T(8,128)(2,1)S(1)} %get-tuple-element.137), channel_id=1, source_target_pairs={{0,1},{1,2},{2,3},{4,5},{5,6},{6,7},{8,9},{9,10},{10,11},{12,13},{... | collective-permute-start | bytes 61448 | tf_op jit(solution)/shard_map/ppermute | solution.py:21
Sparse Core Ops, SparseCore 0:
  120.8 135.3 all-reduce.6
where the time goes:
time: 269 us; the launch traced here: 267 us
  waiting for transfers between devices  135 us (50%)
  starting transfers between devices  47.7 us (18%)
  local copies, waits for them, and re-layouts  44.5 us (17%)
  between operations  15.9 us (6%)
  other arithmetic  13.8 us (5%)
  matrix products  10.3 us (4%)
    psum x1, waiting for transfers between devices, body(): first_sum, second_sum = lax.psum((first_total, second_total), ('gz', 'gy'))  127 us
    ppermute x8, starting transfers between devices, padded_2(): lax.ppermute(tail, axis, [(i, (i + 1) % count) for i in range(ends)])  37.4 us
    concatenate x4, local copies, waits for them, and re-layouts, patch_of(): return jnp.concatenate(pieces, axis=0)  20.4 us
    ppermute x8, starting transfers between devices, padded_2(): lax.ppermute(head, axis, [((i + 1) % count, i) for i in range(ends)])  10.3 us
    slice x8, local copies, waits for them, and re-layouts, patch_of(): cube[:, depth:depth + E, height:height + E, across:across + E]  8.79 us
    ppermute x8, waiting for transfers between devices, padded_2(): lax.ppermute(tail, axis, [(i, (i + 1) % count) for i in range(ends)])  7.11 us
  transfers between devices with their start and end apart: 17, of which 8 were waited for; matrix products, arithmetic and copies ran while one was open for 10% of the time, Pallas kernels for 0%

commit v1 on v0

v1 whole, which is shorter than its diff:
```python
import functools
import math

import jax
import jax.numpy as jnp
from jax import lax
from jax.experimental import pallas as pl
from jax.experimental.pallas import tpu as pltpu
from jax.sharding import PartitionSpec as P

E = 8
VOX = E**3
CH = 64
BX = 2
MESH = pl.DeviceIdType.MESH
F32 = jnp.float32
BF16 = jnp.bfloat16
FACES = ((-1, 0), (1, 0), (0, -1), (0, 1))
EDGES = ((-1, -1), (-1, 1), (1, -1), (1, 1))
PAIR = 2
TILES = 7


def sigmoid(value):
    return 1.0 / (1.0 + jnp.exp(-value))


def kernel(
    n_gz, n_gy,
    place_ref, count_ref, x_ref, ct_ref, w1_ref, w2_ref,
    out_ref, gin_ref, g1_ref, g2_ref,
    qx, qa, qg, wt1, wt2, wf1, wf2, pre_s, gs_s, masks,
    hf_send, hf_recv, he_send, he_recv,
    t_send, t_recv, z_recv, gath,
    hf_ss, hf_rs, he_ss, he_rs, t_ss, t_rs, z_ss, z_rs, g_ss, g_rs,
):
    gz = lax.axis_index("gz")
    gy = lax.axis_index("gy")
    members = PAIR * n_gy
    groups = n_gz // PAIR
    mine = (gz % PAIR) * n_gy + gy
    group = gz // PAIR

    def exists(dz, dy):
        ok = None
        for pos, step, count in ((gz, dz, n_gz), (gy, dy, n_gy)):
            if step:
                here = pos + step >= 0 if step < 0 else pos + step < count
                ok = here if ok is None else jnp.logical_and(ok, here)
        return ok

    def member_id(index):
        return (group * PAIR + index // n_gy, index % n_gy)

    def group_id(index):
        return (index * PAIR + gz % PAIR, gy)

    hf_recv[...] = jnp.zeros_like(hf_recv)
    he_recv[...] = jnp.zeros_like(he_recv)
    barrier = pltpu.get_barrier_semaphore()
    total = jnp.int32(members - 1 + groups - 1)
    for dz, dy in FACES + EDGES:
        ok = exists(dz, dy)
        total = total + ok.astype(jnp.int32)

        @pl.when(ok)
        def _(dz=dz, dy=dy):
            pl.semaphore_signal(barrier, inc=1, device_id=(gz + dz, gy + dy), device_id_type=MESH)

    for r in range(1, members):
        pl.semaphore_signal(barrier, inc=1, device_id=member_id((mine + r) % members), device_id_type=MESH)
    for r in range(1, groups):
        pl.semaphore_signal(barrier, inc=1, device_id=group_id((group + r) % groups), device_id_type=MESH)

    place = jnp.full((E, 128), place_ref[0], jnp.int32).astype(F32)
    live = jnp.full((E, 128), count_ref[0], jnp.int32).astype(F32)
    live = jnp.where(live > 0.5, 1.0, 0.0)
    lane = lax.broadcasted_iota(jnp.int32, (E, 128), 1)
    row = lax.broadcasted_iota(jnp.int32, (E, 128), 0)
    low = lane < CH

    def dup_t(block):
        return jnp.concatenate([block, block], axis=0).T

    def alive(value):
        return (value.reshape(-1, E, 128) * live[None]).reshape(value.shape)

    def x3(value):
        left = pltpu.roll(value, 1, 1)
        right = pltpu.roll(value, E - 1, 1)
        first = jnp.where(low[None], left, value)
        return jnp.concatenate([first, right], axis=-1)

    def halo_copy(e, kind, index):
        offsets, sends, recvs, ss, rs, rows = (
            (FACES, hf_send, hf_recv, hf_ss, hf_rs, 80 if e == 0 else 64)
            if kind == 0
            else (EDGES, he_send, he_recv, he_ss, he_rs, 16)
        )
        dz, dy = offsets[index]
        slot = offsets.index((-dz, -dy))
        return pltpu.make_async_remote_copy(
            src_ref=sends.at[e, index, pl.ds(0, rows)],
            dst_ref=recvs.at[e, slot, pl.ds(0, rows)],
            send_sem=ss.at[e, index],
            recv_sem=rs.at[e, slot],
            device_id=(gz + dz, gy + dy),
            device_id_type=MESH,
        )

    def halo_send(e, value):
        cube = value.reshape(E, E, E, 128)
        for index, (dz, dy) in enumerate(FACES):
            face = cube[0 if dz < 0 else E - 1] if dz else cube[:, 0 if dy < 0 else E - 1]
            face = face.reshape(64, 128)
            hf_send[e, index, 0:64, :] = face.astype(BF16)
            if e == 0:
                hf_send[e, index, 64:80, :] = jnp.concatenate([place, place], axis=0).astype(BF16)
        for index, (dz, dy) in enumerate(EDGES):
            edge = cube[0 if dz < 0 else E - 1, 0 if dy < 0 else E - 1]
            he_send[e, index] = jnp.concatenate([edge, place], axis=0).astype(BF16)
        if e == 0:
            pl.semaphore_wait(barrier, total)
        for kind, offsets in ((0, FACES), (1, EDGES)):
            for index, (dz, dy) in enumerate(offsets):

                @pl.when(exists(dz, dy))
                def _(kind=kind, index=index):
                    halo_copy(e, kind, index).start()

    def halo_wait(e):
        for kind, offsets in ((0, FACES), (1, EDGES)):
            for index, (dz, dy) in enumerate(offsets):

                @pl.when(exists(dz, dy))
                def _(kind=kind, offsets=offsets, dz=dz, dy=dy):
                    halo_copy(e, kind, offsets.index((-dz, -dy))).wait_recv()

    def sends_done(e):
        for kind, offsets in ((0, FACES), (1, EDGES)):
            for index, (dz, dy) in enumerate(offsets):

                @pl.when(exists(dz, dy))
                def _(kind=kind, index=index):
                    halo_copy(e, kind, index).wait_send()

    target0 = jnp.where(jnp.logical_and(low, row == 0), -1.0, 0.0)
    target1 = jnp.where(low, jnp.where(row == E - 1, 1.0, 0.0), 99.0)

    def x_mask(delta):
        return jnp.concatenate(
            [jnp.where(delta == target0, 1.0, 0.0), jnp.where(delta == target1, 1.0, 0.0)], axis=-1
        )

    own_mask = x_mask(jnp.zeros((E, 128), F32))
    own_y = jnp.where(place >= 1.5, 1.0, 0.0)
    own_x = place - 2.0 * own_y

    def make_masks():
        def of(theirs):
            their_y = jnp.where(theirs >= 1.5, 1.0, 0.0)
            return their_y, x_mask(theirs - 2.0 * their_y - own_x)

        def chosen(which, mask):
            keep = jnp.where(which, 1.0, 0.0)
            return mask * jnp.concatenate([keep, keep], axis=-1)

        for s in range(2):
            their_y, mask = of(hf_recv[0, s, 64:80, :].astype(F32)[0:E])
            for n, step in enumerate((-1.0, 0.0, 1.0)):
                masks[3 * s + n] = chosen(their_y - own_y == step, mask)
        for t in range(2):
            dy = 2.0 * t - 1.0
            their_y, mask = of(hf_recv[0, 2 + t, 64:80, :].astype(F32)[0:E])
            masks[6 + t] = chosen(2.0 * dy + their_y - own_y == dy, mask)
            for s in range(2):
                their_y, mask = of(he_recv[0, 2 * s + t].astype(F32)[E : 2 * E])
                masks[8 + 2 * s + t] = chosen(2.0 * dy + their_y - own_y == dy, mask)

    def fill_inside(q, value):
        q[1 : E + 1, 1 : E + 1] = (x3(value.reshape(64, E, 128)) * own_mask[None]).reshape(E, E, E, 256)

    def fill_halo(e, q):
        for s in range(2):
            plane = s * (E + 1)
            spread = x3(hf_recv[e, s, 0:64, :].astype(F32).reshape(E, E, 128))
            q[plane, 1 : E + 1] = spread * masks[3 * s + 1][None]
            for t in range(2):
                edge = he_recv[e, 2 * s + t].astype(F32)[0:E]
                edge = x3(edge[None])[0] * masks[8 + 2 * s + t]
                near = spread[E - 1 if t == 0 else 0] * masks[3 * s + 2 * t]
                q[plane, t * (E + 1)] = edge + near
        for t in range(2):
            spread = x3(hf_recv[e, 2 + t, 0:64, :].astype(F32).reshape(E, E, 128))
            q[1 : E + 1, t * (E + 1)] = spread * masks[6 + t][None]

    def patch(q, k):
        return q[k // 3 : k // 3 + E, k % 3 : k % 3 + E].reshape(VOX, 256).astype(BF16)

    def conv(q, w):
        acc = None
        for k in range(9):
            part = jnp.dot(patch(q, k), w[192 * k : 192 * k + 256, :], preferred_element_type=F32)
            acc = part if acc is None else acc + part
        return acc

    def turn_weight(w_ref, wt):
        for t in range(13):
            wt[128 * t : 128 * t + 128, :] = dup_t(w_ref[:, 128 * t : 128 * t + 128].astype(F32)).astype(BF16)
        wt[1664:1728, :] = dup_t(w_ref[:, 1664:1728].astype(F32)).astype(BF16)
        wt[1728:1792, :] = jnp.zeros((64, 128), BF16)

    def flip_weight(w_ref, wf):
        low64 = lax.broadcasted_iota(jnp.int32, (64, 128), 1) < CH
        for t in range(13):
            tile = w_ref[:, 128 * t : 128 * t + 128].astype(F32)
            turned = pltpu.roll(tile, 64, 1)
            at = (26 - 2 * t) * 64
            wf[at : at + 64, :] = jnp.where(low64, tile, turned).astype(BF16)
            wf[at - 64 : at, :] = jnp.where(low64, turned, tile).astype(BF16)
        last = w_ref[:, 1664:1728].astype(F32)
        wf[0:64, :] = jnp.concatenate([last, last], axis=1).astype(BF16)
        wf[1728:1792, :] = jnp.zeros((64, 128), BF16)

    def terms(g, grads, q):
        turned = grads.T[0:CH].astype(BF16)

        def put(t, tile):
            for r in range(4):
                t_send[g, 2 * r + t // TILES, :, 128 * (t % TILES) : 128 * (t % TILES) + 128] = tile[
                    16 * r : 16 * r + 16
                ].astype(BF16)

        for m in range(5):
            even = jnp.dot(turned, patch(q, 2 * m), preferred_element_type=F32)
            put(3 * m, even[:, 0:128])
            if m == 4:
                put(3 * m + 1, even[:, 128:256])
            else:
                odd = jnp.dot(turned, patch(q, 2 * m + 1), preferred_element_type=F32)
                odd = pltpu.roll(odd, 64, 1)
                put(3 * m + 1, even[:, 128:256] + odd[:, 0:128])
                put(3 * m + 2, odd[:, 128:256])

    def t_copy(g, r):
        to = (mine + r) % members
        return pltpu.make_async_remote_copy(
            src_ref=t_send.at[g, to], dst_ref=t_recv.at[g, mine],
            send_sem=t_ss.at[g, r], recv_sem=t_rs.at[g, r],
            device_id=member_id(to), device_id_type=MESH,
        )

    def z_copy(g, r):
        return pltpu.make_async_remote_copy(
            src_ref=z_recv.at[g, group], dst_ref=z_recv.at[g, group],
            send_sem=z_ss.at[g, r], recv_sem=z_rs.at[g, r],
            device_id=group_id((group + r) % groups), device_id_type=MESH,
        )

    def g_copy(g, r):
        return pltpu.make_async_remote_copy(
            src_ref=gath.at[g, mine], dst_ref=gath.at[g, mine],
            send_sem=g_ss.at[g, r], recv_sem=g_rs.at[g, r],
            device_id=member_id((mine + r) % members), device_id_type=MESH,
        )

    def recv_of(buffer, g, slot, ss, rs, r):
        return pltpu.make_async_remote_copy(
            src_ref=buffer.at[g, slot], dst_ref=buffer.at[g, slot],
            send_sem=ss.at[g, r], recv_sem=rs.at[g, r],
            device_id=member_id((mine + 1) % members), device_id_type=MESH,
        )

    def add_up(buffer, g, count):
        acc = buffer[g, 0].astype(F32)
        for n in range(1, count):
            acc = acc + buffer[g, n].astype(F32)
        return acc.astype(BF16)

    def scatter_start(g):
        for r in range(1, members):
            t_copy(g, r).start()
        t_recv[g, mine] = t_send[g, mine]

    def exchange_start(g):
        for r in range(1, members):
            recv_of(t_recv, g, (mine + members - r) % members, t_ss, t_rs, r).wait_recv()
        z_recv[g, group] = add_up(t_recv, g, members)
        for r in range(1, groups):
            z_copy(g, r).start()

    def gather_start(g):
        for r in range(1, groups):
            recv_of(z_recv, g, (group + groups - r) % groups, z_ss, z_rs, r).wait_recv()
        gath[g, mine] = add_up(z_recv, g, groups)
        for r in range(1, members):
            g_copy(g, r).start()

    def gather_end(g, ref):
        for r in range(1, members):
            recv_of(gath, g, (mine + members - r) % members, g_ss, g_rs, r).wait_recv()
        for r in range(4):
            ref[16 * r : 16 * r + 16, 0:896] = gath[g, 2 * r]
            ref[16 * r : 16 * r + 16, 896:1728] = gath[g, 2 * r + 1][:, 0:832]
        for r in range(1, members):
            t_copy(g, r).wait_send()
            g_copy(g, r).wait_send()
        for r in range(1, groups):
            z_copy(g, r).wait_send()

    x = dup_t(x_ref[...].astype(F32))
    field = alive(x)
    halo_send(0, field)
    fill_inside(qx, field)
    turn_weight(w1_ref, wt1)
    halo_wait(0)
    make_masks()
    fill_halo(0, qx)
    pre = conv(qx, wt1)
    pre_s[...] = pre
    act = alive(pre * sigmoid(pre)).astype(BF16).astype(F32)

    halo_send(1, act)
    fill_inside(qa, act)
    turn_weight(w2_ref, wt2)
    ct = dup_t(ct_ref[...].astype(F32))
    halo_wait(1)
    fill_halo(1, qa)
    summed = dup_t(x_ref[...].astype(F32)) + conv(qa, wt2)
    sig = sigmoid(summed)
    gs = alive(ct * (sig * (1.0 + summed * (1.0 - sig)))).astype(BF16).astype(F32)

    halo_send(2, gs)
    gs_s[...] = gs
    terms(0, gs, qa)
    scatter_start(0)
    out_ref[...] = alive(summed * sig).T[0:CH].astype(BF16)
    fill_inside(qg, gs)
    flip_weight(w2_ref, wf2)
    halo_wait(2)
    fill_halo(2, qg)
    act_grad = conv(qg, wf2)
    pre = pre_s[...]
    sig = sigmoid(pre)
    pg = alive(act_grad * (sig * (1.0 + pre * (1.0 - sig)))).astype(BF16).astype(F32)

    halo_send(3, pg)
    terms(1, pg, qx)
    scatter_start(1)
    exchange_start(0)
    fill_inside(qg, pg)
    flip_weight(w1_ref, wf1)
    exchange_start(1)
    gather_start(0)
    halo_wait(3)
    fill_halo(3, qg)
    gin = alive(gs_s[...] + conv(qg, wf1))
    gather_start(1)
    gin_ref[...] = gin.T[0:CH].astype(BF16)
    gather_end(0, g2_ref)
    gather_end(1, g1_ref)
    for e in range(4):
        sends_done(e)


def body(features, cotangent, first_weight, second_weight, positions, counts):
    n_gz = lax.axis_size("gz")
    n_gy = lax.axis_size("gy")
    slots = features.shape[2]
    scale = 1.0 / math.sqrt(n_gz * n_gy * slots * VOX)
    members = PAIR * n_gy
    groups = n_gz // PAIR
    vmem = pl.BlockSpec(memory_space=pltpu.VMEM)
    smem = pl.BlockSpec(memory_space=pltpu.SMEM)
    dma = pltpu.SemaphoreType.DMA
    output, input_grad, first_sum, second_sum = pl.pallas_call(
        functools.partial(kernel, n_gz, n_gy),
        out_shape=(
            jax.ShapeDtypeStruct((CH, VOX), BF16),
            jax.ShapeDtypeStruct((CH, VOX), BF16),
            jax.ShapeDtypeStruct((CH, 27 * CH), BF16),
            jax.ShapeDtypeStruct((CH, 27 * CH), BF16),
        ),
        in_specs=[smem, smem, vmem, vmem, vmem, vmem],
        out_specs=(vmem,) * 4,
        scratch_shapes=[
            pltpu.VMEM((E + 2, E + 2, E, 256), F32),
            pltpu.VMEM((E + 2, E + 2, E, 256), F32),
            pltpu.VMEM((E + 2, E + 2, E, 256), F32),
            pltpu.VMEM((1792, 128), BF16),
            pltpu.VMEM((1792, 128), BF16),
            pltpu.VMEM((1792, 128), BF16),
            pltpu.VMEM((1792, 128), BF16),
            pltpu.VMEM((VOX, 128), F32),
            pltpu.VMEM((VOX, 128), F32),
            pltpu.VMEM((12, E, 256), F32),
            pltpu.VMEM((4, 4, 80, 128), BF16),
            pltpu.VMEM((4, 4, 80, 128), BF16),
            pltpu.VMEM((4, 4, 16, 128), BF16),
            pltpu.VMEM((4, 4, 16, 128), BF16),
            pltpu.VMEM((2, members, 16, 128 * TILES), BF16),
            pltpu.VMEM((2, members, 16, 128 * TILES), BF16),
            pltpu.VMEM((2, groups, 16, 128 * TILES), BF16),
            pltpu.VMEM((2, members, 16, 128 * TILES), BF16),
            dma((4, 4)), dma((4, 4)), dma((4, 4)), dma((4, 4)),
            dma((2, members)), dma((2, members)),
            dma((2, groups)), dma((2, groups)),
            dma((2, members)), dma((2, members)),
        ],
        compiler_params=pltpu.CompilerParams(collective_id=0, has_side_effects=True),
    )(
        positions.reshape(1), counts.reshape(1), features[0, 0, 0], cotangent[0, 0, 0],
        first_weight, second_weight,
    )
    first_grad = first_sum.astype(F32) * scale
    second_grad = second_sum.astype(F32) * scale
    return (output[None, None, None], input_grad[None, None, None], first_grad, second_grad)


def solution(mesh):
    return jax.shard_map(
        body,
        mesh=mesh,
        in_specs=(
            P("gz", "gy", None, None, None),
            P("gz", "gy", None, None, None),
            P(),
            P(),
            P("gz", "gy", None),
            P("gz", "gy"),
        ),
        out_specs=(P("gz", "gy", None, None, None), P("gz", "gy", None, None, None), P(), P()),
        check_vma=False,
    )
```

time: 269 us -> 43.1 us (0.16)
  waiting for transfers between devices: 135 us -> 0 us
  starting transfers between devices: 47.7 us -> 0 us
  local copies, waits for them, and re-layouts: 44.5 us -> 1.5 us
  Pallas kernels: 0 us -> 37.4 us
  between operations: 15.9 us -> 1.94 us
  other arithmetic: 13.8 us -> 2.06 us
  matrix products: 10.3 us -> 0 us
    psum x1 -> x0, waiting for transfers between devices: 127 us -> none  [body(): first_sum, second_sum = lax.psum((first_total, second_total), ('gz', 'gy'))]
    ppermute x16 -> x0, starting transfers between devices: 47.7 us -> none  [the longest x8 37.4 us: padded_2(): lax.ppermute(tail, axis, [(i, (i + 1) % count) for i in range(ends)])]
    pallas_call x0 -> x1, Pallas kernels: none -> 37.4 us  [body(): pl.pallas_call(functools.partial(kernel, n_gz, n_gy), out_shape=(jax.Shap...]
    concatenate x4 -> x0, local copies, waits for them, and re-layouts: 20.4 us -> none  [patch_of(): return jnp.concatenate(pieces, axis=0)]
    dot_general x6 -> x0, matrix products: 10.3 us -> none  [the longest x2 3.93 us: step(): lax.dot_general(grad_here, patch_of(other_pad, place), (((1,), (1,)), (()...]
    slice x12 -> x0, local copies, waits for them, and re-layouts: 9.49 us -> none  [the longest x8 8.79 us: patch_of(): cube[:, depth:depth + E, height:height + E, across:across + E]]
    ppermute x16 -> x0, waiting for transfers between devices: 7.75 us -> none  [the longest x8 7.11 us: padded_2(): lax.ppermute(tail, axis, [(i, (i + 1) % count) for i in range(ends)])]
    transpose x6 -> x0, local copies, waits for them, and re-layouts: 5.37 us -> none  [the longest x2 5 us: flip_weight(): return weight.reshape(channels, 27, channels)[:, ::-1, :].transpose(2, 1,...]
  transfers between devices with their start and end apart: 17 -> 0, of which waited for: 8 -> 0; matrix products, arithmetic and copies ran while one was open for 10% -> 0% of each run, Pallas kernels for 0% -> 0%
where the time goes in v1:
time: 43.1 us; the launch traced here: 42.9 us
  Pallas kernels  37.4 us (87%)
  other arithmetic  2.06 us (5%)
  between operations  1.94 us (5%)
  local copies, waits for them, and re-layouts  1.5 us (3%)
    pallas_call x1, Pallas kernels, body(): pl.pallas_call(functools.partial(kernel, n_gz, n_gy), out_shape=(jax.Shap...  37.4 us
    mul x1, other arithmetic, body(): second_grad = second_sum.astype(F32) * scale  2.06 us
    unnamed x6, local copies, waits for them, and re-layouts  1.5 us

profile of v1, /device:TPU:0, one launch (start us, length us, event | category | flops | bytes accessed | tf_op | source)
XLA Modules:
  0.0 42.9 jit_solution(18304312443629876393)
XLA Ops:
  1.9 37.4 %shard_map.93 = (bf16[64,512]{1,0:T(8,128)(2,1)}, bf16[64,512]{1,0:T(8,128)(2,1)}, bf16[64,1728]{1,0:T(8,128)(2,1)}, bf16[64,1728]{1,0:T(8,128)(2,1)}) custom-call(s32[1]{0:T(128)} %bitcast.6.place_ref, s32[1]{0:T(128)} %bitcast.7.count_ref, bf16[64,512]{1,0:T(8,128)(2,1)} %bitcast.8, bf16[64,512]{1,0:T(8,128)(2,1)} %bitcast.9, bf16[64,1728]{1,0:T(8,128)(2,1)} %w1_ref.1, ...), custom_call_target="tpu_custom_call" | custom-call | tf_op jit(solution)/shard_map/pallas_call | solution.py:376
  39.4 0.0 copy-start.1
  39.4 2.1 %convert_multiply_fusion = (f32[64,1728]{1,0:T(8,128)}, f32[64,1728]{1,0:T(8,128)}) fusion(bf16[64,1728]{1,0:T(8,128)(2,1)} %get-tuple-element.11, bf16[64,1728]{1,0:T(8,128)(2,1)} %get-tuple-element.10), kind=kLoop, calls=%fused_computation | loop fusion | flops 442368 | bytes 1327104 | tf_op jit(solution)/shard_map/mul | solution.py:416
  41.4 0.0 copy-done.1
  41.4 0.0 copy-start
  41.4 0.6 %copy.14 = bf16[1,1,1,64,512]{4,3,2,1,0:T(8,128)(2,1)} copy(bf16[1,1,1,64,512]{4,3,2,1,0:T(8,128)(2,1)S(1)} %bitcast.11) | data formatting | bytes 131072
  42.1 0.2 copy-done
  42.3 0.6 %copy.15 = bf16[1,1,1,64,512]{4,3,2,1,0:T(8,128)(2,1)} copy(bf16[1,1,1,64,512]{4,3,2,1,0:T(8,128)(2,1)S(1)} %bitcast.10) | data formatting | bytes 131072
Async XLA Ops:
  39.4 2.1 %copy-start.1 = (bf16[64,512]{1,0:T(8,128)(2,1)S(1)}, bf16[64,512]{1,0:T(8,128)(2,1)}, u32[]{:S(2)}) copy-start(bf16[64,512]{1,0:T(8,128)(2,1)} %get-tuple-element.8) | copy-start | bytes 196612
  41.4 0.9 %copy-start = (bf16[64,512]{1,0:T(8,128)(2,1)S(1)}, bf16[64,512]{1,0:T(8,128)(2,1)}, u32[]{:S(2)}) copy-start(bf16[64,512]{1,0:T(8,128)(2,1)} %get-tuple-element.9) | copy-start | bytes 196612

commit v2 on v1

--- a/solution.py
+++ b/solution.py
@@ -19,6 +19,7 @@
 EDGES = ((-1, -1), (-1, 1), (1, -1), (1, 1))
 PAIR = 2
 TILES = 7
+UNITS = ((0, 0, 896), (1, 0, 512), (1, 512, 896))
 
 
 def sigmoid(value):
@@ -29,7 +30,7 @@
     n_gz, n_gy,
     place_ref, count_ref, x_ref, ct_ref, w1_ref, w2_ref,
     out_ref, gin_ref, g1_ref, g2_ref,
-    qx, qa, qg, wt1, wt2, wf1, wf2, pre_s, gs_s, masks,
+    qx, qa, qg, qp, acc, wt1, wt2, wf1, wf2, pre_s, gs_s, masks,
     hf_send, hf_recv, he_send, he_recv,
     t_send, t_recv, z_recv, gath,
     hf_ss, hf_rs, he_ss, he_rs, t_ss, t_rs, z_ss, z_rs, g_ss, g_rs,
@@ -128,13 +129,20 @@
                 def _(kind=kind, index=index):
                     halo_copy(e, kind, index).start()
 
-    def halo_wait(e):
-        for kind, offsets in ((0, FACES), (1, EDGES)):
-            for index, (dz, dy) in enumerate(offsets):
-
-                @pl.when(exists(dz, dy))
-                def _(kind=kind, offsets=offsets, dz=dz, dy=dy):
-                    halo_copy(e, kind, offsets.index((-dz, -dy))).wait_recv()
+    def arrive(e, kind, offsets, index):
+        dz, dy = offsets[index]
+
+        @pl.when(exists(dz, dy))
+        def _():
+            halo_copy(e, kind, offsets.index((-dz, -dy))).wait_recv()
+
+    def face_wait(e, indices):
+        for index in indices:
+            arrive(e, 0, FACES, index)
+
+    def edge_wait(e):
+        for index in range(4):
+            arrive(e, 1, EDGES, index)
 
     def sends_done(e):
         for kind, offsets in ((0, FACES), (1, EDGES)):
@@ -156,7 +164,7 @@
     own_y = jnp.where(place >= 1.5, 1.0, 0.0)
     own_x = place - 2.0 * own_y
 
-    def make_masks():
+    def make_masks(part):
         def of(theirs):
             their_y = jnp.where(theirs >= 1.5, 1.0, 0.0)
             return their_y, x_mask(theirs - 2.0 * their_y - own_x)
@@ -165,44 +173,81 @@
             keep = jnp.where(which, 1.0, 0.0)
             return mask * jnp.concatenate([keep, keep], axis=-1)
 
-        for s in range(2):
-            their_y, mask = of(hf_recv[0, s, 64:80, :].astype(F32)[0:E])
-            for n, step in enumerate((-1.0, 0.0, 1.0)):
-                masks[3 * s + n] = chosen(their_y - own_y == step, mask)
+        if part == 0:
+            for s in range(2):
+                their_y, mask = of(hf_recv[0, s, 64:80, :].astype(F32)[0:E])
+                for n, step in enumerate((-1.0, 0.0, 1.0)):
+                    masks[3 * s + n] = chosen(their_y - own_y == step, mask)
         for t in range(2):
             dy = 2.0 * t - 1.0
-            their_y, mask = of(hf_recv[0, 2 + t, 64:80, :].astype(F32)[0:E])
-            masks[6 + t] = chosen(2.0 * dy + their_y - own_y == dy, mask)
-            for s in range(2):
-                their_y, mask = of(he_recv[0, 2 * s + t].astype(F32)[E : 2 * E])
-                masks[8 + 2 * s + t] = chosen(2.0 * dy + their_y - own_y == dy, mask)
+            if part == 1:
+                their_y, mask = of(hf_recv[0, 2 + t, 64:80, :].astype(F32)[0:E])
+                masks[6 + t] = chosen(2.0 * dy + their_y - own_y == dy, mask)
+            if part == 2:
+                for s in range(2):
+                    their_y, mask = of(he_recv[0, 2 * s + t].astype(F32)[E : 2 * E])
+                    masks[8 + 2 * s + t] = chosen(2.0 * dy + their_y - own_y == dy, mask)
 
     def fill_inside(q, value):
         q[1 : E + 1, 1 : E + 1] = (x3(value.reshape(64, E, 128)) * own_mask[None]).reshape(E, E, E, 256)
 
-    def fill_halo(e, q):
+    def patch(q, k):
+        return q[k // 3 : k // 3 + E, k % 3 : k % 3 + E].reshape(VOX, 256).astype(BF16)
+
+    def clear_halo(q):
+        for plane in (0, E + 1):
+            q[plane] = jnp.zeros((E + 2, E, 256), F32)
+            q[1 : E + 1, plane] = jnp.zeros((E, E, 256), F32)
+
+    def rows_of(w, k):
+        return w[192 * k : 192 * k + 256, :]
+
+    def conv_inside(q, w):
+        total = None
+        for k in range(9):
+            part = jnp.dot(patch(q, k), rows_of(w, k), preferred_element_type=F32)
+            total = part if total is None else total + part
+        acc[...] = total.reshape(E, E, E, 128)
+
+    def conv_halo(e, q, w):
+        def side(pieces):
+            total = None
+            for piece, k in pieces:
+                part = jnp.dot(piece.reshape(64, 256).astype(BF16), rows_of(w, k), preferred_element_type=F32)
+                total = part if total is None else total + part
+            return total.reshape(E, E, 128)
+
+        face_wait(e, (2, 3))
+        if e == 0:
+            make_masks(1)
+        for t in range(2):
+            spread = x3(hf_recv[e, 2 + t, 0:64, :].astype(F32).reshape(E, E, 128))
+            q[1 : E + 1, t * (E + 1)] = spread * masks[6 + t][None]
+            acc[:, t * (E - 1)] += side(
+                [(q[dz : dz + E, t * (E + 1)], 3 * dz + 2 * t) for dz in range(3)]
+            )
+        face_wait(e, (0, 1))
+        if e == 0:
+            make_masks(0)
         for s in range(2):
             plane = s * (E + 1)
             spread = x3(hf_recv[e, s, 0:64, :].astype(F32).reshape(E, E, 128))
             q[plane, 1 : E + 1] = spread * masks[3 * s + 1][None]
             for t in range(2):
+                q[plane, t * (E + 1)] = spread[E - 1 if t == 0 else 0] * masks[3 * s + 2 * t]
+            acc[s * (E - 1)] += side([(q[plane, dy : dy + E], 6 * s + dy) for dy in range(3)])
+        edge_wait(e)
+        if e == 0:
+            make_masks(2)
+        for s in range(2):
+            for t in range(2):
                 edge = he_recv[e, 2 * s + t].astype(F32)[0:E]
                 edge = x3(edge[None])[0] * masks[8 + 2 * s + t]
-                near = spread[E - 1 if t == 0 else 0] * masks[3 * s + 2 * t]
-                q[plane, t * (E + 1)] = edge + near
-        for t in range(2):
-            spread = x3(hf_recv[e, 2 + t, 0:64, :].astype(F32).reshape(E, E, 128))
-            q[1 : E + 1, t * (E + 1)] = spread * masks[6 + t][None]
-
-    def patch(q, k):
-        return q[k // 3 : k // 3 + E, k % 3 : k % 3 + E].reshape(VOX, 256).astype(BF16)
-
-    def conv(q, w):
-        acc = None
-        for k in range(9):
-            part = jnp.dot(patch(q, k), w[192 * k : 192 * k + 256, :], preferred_element_type=F32)
-            acc = part if acc is None else acc + part
-        return acc
+                q[s * (E + 1), t * (E + 1)] += edge
+                acc[s * (E - 1), t * (E - 1)] += jnp.dot(
+                    edge.astype(BF16), rows_of(w, 6 * s + 2 * t), preferred_element_type=F32
+                )
+        return acc[...].reshape(VOX, 128)
 
     def turn_weight(w_ref, wt):
         for t in range(13):
@@ -242,91 +287,104 @@
                 put(3 * m + 1, even[:, 128:256] + odd[:, 0:128])
                 put(3 * m + 2, odd[:, 128:256])
 
-    def t_copy(g, r):
+    def part_of(buffer, u, slot):
+        g, lo, hi = UNITS[u]
+        return buffer.at[g, slot, :, lo:hi]
+
+    def t_copy(u, r):
         to = (mine + r) % members
         return pltpu.make_async_remote_copy(
-            src_ref=t_send.at[g, to], dst_ref=t_recv.at[g, mine],
-            send_sem=t_ss.at[g, r], recv_sem=t_rs.at[g, r],
+            src_ref=part_of(t_send, u, to), dst_ref=part_of(t_recv, u, mine),
+            send_sem=t_ss.at[u, r], recv_sem=t_rs.at[u, r],
             device_id=member_id(to), device_id_type=MESH,
         )
 
-    def z_copy(g, r):
+    def z_copy(u, r):
         return pltpu.make_async_remote_copy(
-            src_ref=z_recv.at[g, group], dst_ref=z_recv.at[g, group],
-            send_sem=z_ss.at[g, r], recv_sem=z_rs.at[g, r],
+            src_ref=part_of(z_recv, u, group), dst_ref=part_of(z_recv, u, group),
+            send_sem=z_ss.at[u, r], recv_sem=z_rs.at[u, r],
             device_id=group_id((group + r) % groups), device_id_type=MESH,
         )
 
-    def g_copy(g, r):
+    def g_copy(u, r):
         return pltpu.make_async_remote_copy(
-            src_ref=gath.at[g, mine], dst_ref=gath.at[g, mine],
-            send_sem=g_ss.at[g, r], recv_sem=g_rs.at[g, r],
+            src_ref=part_of(gath, u, mine), dst_ref=part_of(gath, u, mine),
+            send_sem=g_ss.at[u, r], recv_sem=g_rs.at[u, r],
             device_id=member_id((mine + r) % members), device_id_type=MESH,
         )
 
-    def recv_of(buffer, g, slot, ss, rs, r):
+    def recv_of(buffer, u, slot, ss, rs, r):
         return pltpu.make_async_remote_copy(
-            src_ref=buffer.at[g, slot], dst_ref=buffer.at[g, slot],
-            send_sem=ss.at[g, r], recv_sem=rs.at[g, r],
+            src_ref=part_of(buffer, u, slot), dst_ref=part_of(buffer, u, slot),
+            send_sem=ss.at[u, r], recv_sem=rs.at[u, r],
             device_id=member_id((mine + 1) % members), device_id_type=MESH,
         )
 
-    def add_up(buffer, g, count):
-        acc = buffer[g, 0].astype(F32)
+    def add_up(buffer, u, count):
+        g, lo, hi = UNITS[u]
+        total = buffer[g, 0, :, lo:hi].astype(F32)
         for n in range(1, count):
-            acc = acc + buffer[g, n].astype(F32)
-        return acc.astype(BF16)
-
-    def scatter_start(g):
+            total = total + buffer[g, n, :, lo:hi].astype(F32)
+        return total.astype(BF16)
+
+    def scatter_start(u):
+        g, lo, hi = UNITS[u]
         for r in range(1, members):
-            t_copy(g, r).start()
-        t_recv[g, mine] = t_send[g, mine]
-
-    def exchange_start(g):
+            t_copy(u, r).start()
+        t_recv[g, mine, :, lo:hi] = t_send[g, mine, :, lo:hi]
+
+    def exchange_start(u):
+        g, lo, hi = UNITS[u]
         for r in range(1, members):
-            recv_of(t_recv, g, (mine + members - r) % members, t_ss, t_rs, r).wait_recv()
-        z_recv[g, group] = add_up(t_recv, g, members)
+            recv_of(t_recv, u, (mine + members - r) % members, t_ss, t_rs, r).wait_recv()
+        z_recv[g, group, :, lo:hi] = add_up(t_recv, u, members)
         for r in range(1, groups):
-            z_copy(g, r).start()
-
-    def gather_start(g):
+            z_copy(u, r).start()
+
+    def gather_start(u):
+        g, lo, hi = UNITS[u]
         for r in range(1, groups):
-            recv_of(z_recv, g, (group + groups - r) % groups, z_ss, z_rs, r).wait_recv()
-        gath[g, mine] = add_up(z_recv, g, groups)
+            recv_of(z_recv, u, (group + groups - r) % groups, z_ss, z_rs, r).wait_recv()
+        gath[g, mine, :, lo:hi] = add_up(z_recv, u, groups)
         for r in range(1, members):
-            g_copy(g, r).start()
-
-    def gather_end(g, ref):
+            g_copy(u, r).start()
+
+    def gather_end(u, ref):
+        g, lo, hi = UNITS[u]
         for r in range(1, members):
-            recv_of(gath, g, (mine + members - r) % members, g_ss, g_rs, r).wait_recv()
+            recv_of(gath, u, (mine + members - r) % members, g_ss, g_rs, r).wait_recv()
         for r in range(4):
-            ref[16 * r : 16 * r + 16, 0:896] = gath[g, 2 * r]
-            ref[16 * r : 16 * r + 16, 896:1728] = gath[g, 2 * r + 1][:, 0:832]
+            ref[16 * r : 16 * r + 16, lo:hi] = gath[g, 2 * r, :, lo:hi]
+            end = min(hi, 832)
+            ref[16 * r : 16 * r + 16, 896 + lo : 896 + end] = gath[g, 2 * r + 1, :, lo:end]
+
+    def reduce_done(u):
         for r in range(1, members):
-            t_copy(g, r).wait_send()
-            g_copy(g, r).wait_send()
+            t_copy(u, r).wait_send()
+            g_copy(u, r).wait_send()
         for r in range(1, groups):
-            z_copy(g, r).wait_send()
+            z_copy(u, r).wait_send()
 
     x = dup_t(x_ref[...].astype(F32))
     field = alive(x)
+    fill_inside(qx, field)
+    for q in (qx, qa, qg, qp):
+        clear_halo(q)
+    turn_weight(w1_ref, wt1)
     halo_send(0, field)
-    fill_inside(qx, field)
-    turn_weight(w1_ref, wt1)
-    halo_wait(0)
-    make_masks()
-    fill_halo(0, qx)
-    pre = conv(qx, wt1)
+    conv_inside(qx, wt1)
+    turn_weight(w2_ref, wt2)
+    flip_weight(w2_ref, wf2)
+    pre = conv_halo(0, qx, wt1)
+    act = alive(pre * sigmoid(pre)).astype(BF16).astype(F32)
+
+    halo_send(1, act)
     pre_s[...] = pre
-    act = alive(pre * sigmoid(pre)).astype(BF16).astype(F32)
-
-    halo_send(1, act)
     fill_inside(qa, act)
-    turn_weight(w2_ref, wt2)
+    conv_inside(qa, wt2)
+    flip_weight(w1_ref, wf1)
     ct = dup_t(ct_ref[...].astype(F32))
-    halo_wait(1)
-    fill_halo(1, qa)
-    summed = dup_t(x_ref[...].astype(F32)) + conv(qa, wt2)
+    summed = dup_t(x_ref[...].astype(F32)) + conv_halo(1, qa, wt2)
     sig = sigmoid(summed)
     gs = alive(ct * (sig * (1.0 + summed * (1.0 - sig)))).astype(BF16).astype(F32)
 
@@ -334,12 +392,10 @@
     gs_s[...] = gs
     terms(0, gs, qa)
     scatter_start(0)
+    fill_inside(qg, gs)
+    conv_inside(qg, wf2)
     out_ref[...] = alive(summed * sig).T[0:CH].astype(BF16)
-    fill_inside(qg, gs)
-    flip_weight(w2_ref, wf2)
-    halo_wait(2)
-    fill_halo(2, qg)
-    act_grad = conv(qg, wf2)
+    act_grad = conv_halo(2, qg, wf2)
     pre = pre_s[...]
     sig = sigmoid(pre)
     pg = alive(act_grad * (sig * (1.0 + pre * (1.0 - sig)))).astype(BF16).astype(F32)
@@ -347,20 +403,31 @@
     halo_send(3, pg)
     terms(1, pg, qx)
     scatter_start(1)
+    scatter_start(2)
     exchange_start(0)
-    fill_inside(qg, pg)
-    flip_weight(w1_ref, wf1)
+    fill_inside(qp, pg)
+    conv_inside(qp, wf1)
     exchange_start(1)
+    exchange_start(2)
     gather_start(0)
-    halo_wait(3)
-    fill_halo(3, qg)
-    gin = alive(gs_s[...] + conv(qg, wf1))
+    gin = alive(gs_s[...] + conv_halo(3, qp, wf1))
     gather_start(1)
+    gather_start(2)
     gin_ref[...] = gin.T[0:CH].astype(BF16)
+    for e in range(4):
+        sends_done(e)
     gather_end(0, g2_ref)
     gather_end(1, g1_ref)
-    for e in range(4):
-        sends_done(e)
+    gather_end(2, g1_ref)
+    for u in range(3):
+        reduce_done(u)
+
+
+def finish(scale, out_in, gin_in, g1_in, g2_in, out_ref, gin_ref, g1_ref, g2_ref):
+    out_ref[...] = out_in[...]
+    gin_ref[...] = gin_in[...]
+    g1_ref[...] = g1_in[...].astype(F32) * scale
+    g2_ref[...] = g2_in[...].astype(F32) * scale
 
 
 def body(features, cotangent, first_weight, second_weight, positions, counts):
@@ -387,6 +454,8 @@
             pltpu.VMEM((E + 2, E + 2, E, 256), F32),
             pltpu.VMEM((E + 2, E + 2, E, 256), F32),
             pltpu.VMEM((E + 2, E + 2, E, 256), F32),
+            pltpu.VMEM((E + 2, E + 2, E, 256), F32),
+            pltpu.VMEM((E, E, E, 128), F32),
             pltpu.VMEM((1792, 128), BF16),
             pltpu.VMEM((1792, 128), BF16),
             pltpu.VMEM((1792, 128), BF16),
@@ -403,17 +472,23 @@
             pltpu.VMEM((2, groups, 16, 128 * TILES), BF16),
             pltpu.VMEM((2, members, 16, 128 * TILES), BF16),
             dma((4, 4)), dma((4, 4)), dma((4, 4)), dma((4, 4)),
-            dma((2, members)), dma((2, members)),
-            dma((2, groups)), dma((2, groups)),
-            dma((2, members)), dma((2, members)),
+            dma((3, members)), dma((3, members)),
+            dma((3, groups)), dma((3, groups)),
+            dma((3, members)), dma((3, members)),
         ],
         compiler_params=pltpu.CompilerParams(collective_id=0, has_side_effects=True),
     )(
         positions.reshape(1), counts.reshape(1), features[0, 0, 0], cotangent[0, 0, 0],
         first_weight, second_weight,
     )
-    first_grad = first_sum.astype(F32) * scale
-    second_grad = second_sum.astype(F32) * scale
+    grad = jax.ShapeDtypeStruct((CH, 27 * CH), F32)
+    brick = jax.ShapeDtypeStruct((CH, VOX), BF16)
+    output, input_grad, first_grad, second_grad = pl.pallas_call(
+        functools.partial(finish, scale),
+        out_shape=(brick, brick, grad, grad),
+        in_specs=[vmem] * 4,
+        out_specs=(vmem,) * 4,
+    )(output, input_grad, first_sum, second_sum)
     return (output[None, None, None], input_grad[None, None, None], first_grad, second_grad)
 
 

time: 43.1 us -> 37.9 us (0.88)
  other arithmetic: 2.06 us -> 0 us
  Pallas kernels: 37.4 us -> 35.8 us
  local copies, waits for them, and re-layouts: 1.5 us -> 0 us
    pallas_call x1, Pallas kernels: 37.4 us -> 33.7 us  [body(): pl.pallas_call(functools.partial(kernel, n_gz, n_gy), out_shape=(jax.Shap...]
    pallas_call x0 -> x1, Pallas kernels: none -> 2.09 us  [body(): pl.pallas_call(functools.partial(finish, scale), out_shape=(brick, brick,...]
    mul x1 -> x0, other arithmetic: 2.06 us -> none  [body(): second_grad = second_sum.astype(F32) * scale]
    unnamed x6 -> x0, local copies, waits for them, and re-layouts: 1.5 us -> none
where the time goes in v2:
time: 37.9 us; the launch traced here: 37.7 us
  Pallas kernels  35.8 us (94%)
  between operations  1.93 us (5%)
    pallas_call x1, Pallas kernels, body(): pl.pallas_call(functools.partial(kernel, n_gz, n_gy), out_shape=(jax.Shap...  33.7 us
    pallas_call x1, Pallas kernels, body(): pl.pallas_call(functools.partial(finish, scale), out_shape=(brick, brick,...  2.09 us

profile of v2, /device:TPU:0, one launch (start us, length us, event | category | flops | bytes accessed | tf_op | source)
XLA Modules:
  0.0 37.7 jit_solution(13143755996254425897)
XLA Ops:
  1.9 33.7 %shard_map.93 = (bf16[64,512]{1,0:T(8,128)(2,1)}, bf16[64,512]{1,0:T(8,128)(2,1)}, bf16[64,1728]{1,0:T(8,128)(2,1)}, bf16[64,1728]{1,0:T(8,128)(2,1)}) custom-call(s32[1]{0:T(128)} %bitcast.6.place_ref, s32[1]{0:T(128)} %bitcast.7.count_ref, bf16[64,512]{1,0:T(8,128)(2,1)} %bitcast.8, bf16[64,512]{1,0:T(8,128)(2,1)} %bitcast.9, bf16[64,1728]{1,0:T(8,128)(2,1)} %w1_ref.1, ...), custom_call_target="tpu_custom_call" | custom-call | tf_op jit(solution)/shard_map/pallas_call | solution.py:443
  35.6 2.1 %shard_map.94 = (bf16[64,512]{1,0:T(8,128)(2,1)}, bf16[64,512]{1,0:T(8,128)(2,1)}, f32[64,1728]{1,0:T(8,128)}, f32[64,1728]{1,0:T(8,128)}) custom-call(bf16[64,512]{1,0:T(8,128)(2,1)} %get-tuple-element.12.out_in, bf16[64,512]{1,0:T(8,128)(2,1)} %get-tuple-element.13.gin_in, bf16[64,1728]{1,0:T(8,128)(2,1)} %get-tuple-element.14.g1_in, ...), custom_call_target="tpu_custom_call" | custom-call | tf_op jit(solution)/shard_map/pallas_call | solution.py:486

commit v3 on v2

--- a/solution.py
+++ b/solution.py
@@ -28,8 +28,9 @@
 
 def kernel(
     n_gz, n_gy,
-    place_ref, count_ref, x_ref, ct_ref, w1_ref, w2_ref,
+    place_ref, count_ref, x_hbm, ct_hbm, w1_hbm, w2_hbm,
     out_ref, gin_ref, g1_ref, g2_ref,
+    x_ref, ct_ref, w1_ref, w2_ref, in_sems,
     qx, qa, qg, qp, acc, wt1, wt2, wf1, wf2, pre_s, gs_s, masks,
     hf_send, hf_recv, he_send, he_recv,
     t_send, t_recv, z_recv, gath,
@@ -72,6 +73,15 @@
         pl.semaphore_signal(barrier, inc=1, device_id=member_id((mine + r) % members), device_id_type=MESH)
     for r in range(1, groups):
         pl.semaphore_signal(barrier, inc=1, device_id=group_id((group + r) % groups), device_id_type=MESH)
+
+    loads = [
+        pltpu.make_async_copy(src, dst, in_sems.at[n])
+        for n, (src, dst) in enumerate(
+            ((x_hbm, x_ref), (w1_hbm, w1_ref), (w2_hbm, w2_ref), (ct_hbm, ct_ref))
+        )
+    ]
+    for load in loads:
+        load.start()
 
     place = jnp.full((E, 128), place_ref[0], jnp.int32).astype(F32)
     live = jnp.full((E, 128), count_ref[0], jnp.int32).astype(F32)
@@ -122,7 +132,7 @@
             he_send[e, index] = jnp.concatenate([edge, place], axis=0).astype(BF16)
         if e == 0:
             pl.semaphore_wait(barrier, total)
-        for kind, offsets in ((0, FACES), (1, EDGES)):
+        for kind, offsets in ((1, EDGES), (0, FACES)):
             for index, (dz, dy) in enumerate(offsets):
 
                 @pl.when(exists(dz, dy))
@@ -267,12 +277,12 @@
         wf[0:64, :] = jnp.concatenate([last, last], axis=1).astype(BF16)
         wf[1728:1792, :] = jnp.zeros((64, 128), BF16)
 
-    def terms(g, grads, q):
+    def terms(g, grads, q, ready):
         turned = grads.T[0:CH].astype(BF16)
 
         def put(t, tile):
             for r in range(4):
-                t_send[g, 2 * r + t // TILES, :, 128 * (t % TILES) : 128 * (t % TILES) + 128] = tile[
+                t_send[g, 2 * r + t % 2, :, 128 * (t // 2) : 128 * (t // 2) + 128] = tile[
                     16 * r : 16 * r + 16
                 ].astype(BF16)
 
@@ -286,6 +296,8 @@
                 odd = pltpu.roll(odd, 64, 1)
                 put(3 * m + 1, even[:, 128:256] + odd[:, 0:128])
                 put(3 * m + 2, odd[:, 128:256])
+            if m in ready:
+                scatter_start(ready[m])
 
     def part_of(buffer, u, slot):
         g, lo, hi = UNITS[u]
@@ -354,9 +366,12 @@
         for r in range(1, members):
             recv_of(gath, u, (mine + members - r) % members, g_ss, g_rs, r).wait_recv()
         for r in range(4):
-            ref[16 * r : 16 * r + 16, lo:hi] = gath[g, 2 * r, :, lo:hi]
-            end = min(hi, 832)
-            ref[16 * r : 16 * r + 16, 896 + lo : 896 + end] = gath[g, 2 * r + 1, :, lo:end]
+            for t in range(2 * lo // 128, 2 * hi // 128):
+                end = min(128 * t + 128, 27 * CH)
+                at = 128 * (t // 2)
+                ref[16 * r : 16 * r + 16, 128 * t : end] = gath[
+                    g, 2 * r + t % 2, :, at : at + end - 128 * t
+                ]
 
     def reduce_done(u):
         for r in range(1, members):
@@ -365,24 +380,29 @@
         for r in range(1, groups):
             z_copy(u, r).wait_send()
 
+    for q in (qx, qa, qg, qp):
+        clear_halo(q)
+    loads[0].wait()
     x = dup_t(x_ref[...].astype(F32))
     field = alive(x)
     fill_inside(qx, field)
-    for q in (qx, qa, qg, qp):
-        clear_halo(q)
+    loads[1].wait()
     turn_weight(w1_ref, wt1)
     halo_send(0, field)
     conv_inside(qx, wt1)
+    loads[2].wait()
     turn_weight(w2_ref, wt2)
     flip_weight(w2_ref, wf2)
     pre = conv_halo(0, qx, wt1)
     act = alive(pre * sigmoid(pre)).astype(BF16).astype(F32)
 
     halo_send(1, act)
-    pre_s[...] = pre
+    sig = sigmoid(pre)
+    pre_s[...] = sig * (1.0 + pre * (1.0 - sig))
     fill_inside(qa, act)
     conv_inside(qa, wt2)
     flip_weight(w1_ref, wf1)
+    loads[3].wait()
     ct = dup_t(ct_ref[...].astype(F32))
     summed = dup_t(x_ref[...].astype(F32)) + conv_halo(1, qa, wt2)
     sig = sigmoid(summed)
@@ -390,20 +410,15 @@
 
     halo_send(2, gs)
     gs_s[...] = gs
-    terms(0, gs, qa)
-    scatter_start(0)
+    terms(0, gs, qa, {4: 0})
     fill_inside(qg, gs)
     conv_inside(qg, wf2)
     out_ref[...] = alive(summed * sig).T[0:CH].astype(BF16)
     act_grad = conv_halo(2, qg, wf2)
-    pre = pre_s[...]
-    sig = sigmoid(pre)
-    pg = alive(act_grad * (sig * (1.0 + pre * (1.0 - sig)))).astype(BF16).astype(F32)
-
+    pg = alive(act_grad * pre_s[...]).astype(BF16).astype(F32)
+
+    terms(1, pg, qx, {2: 1, 4: 2})
     halo_send(3, pg)
-    terms(1, pg, qx)
-    scatter_start(1)
-    scatter_start(2)
     exchange_start(0)
     fill_inside(qp, pg)
     conv_inside(qp, wf1)
@@ -440,17 +455,23 @@
     vmem = pl.BlockSpec(memory_space=pltpu.VMEM)
     smem = pl.BlockSpec(memory_space=pltpu.SMEM)
     dma = pltpu.SemaphoreType.DMA
+    hbm = pl.BlockSpec(memory_space=pl.ANY)
     output, input_grad, first_sum, second_sum = pl.pallas_call(
         functools.partial(kernel, n_gz, n_gy),
         out_shape=(
-            jax.ShapeDtypeStruct((CH, VOX), BF16),
-            jax.ShapeDtypeStruct((CH, VOX), BF16),
-            jax.ShapeDtypeStruct((CH, 27 * CH), BF16),
-            jax.ShapeDtypeStruct((CH, 27 * CH), BF16),
+            pltpu.VMEM((CH, VOX), BF16),
+            pltpu.VMEM((CH, VOX), BF16),
+            pltpu.VMEM((CH, 27 * CH), BF16),
+            pltpu.VMEM((CH, 27 * CH), BF16),
         ),
-        in_specs=[smem, smem, vmem, vmem, vmem, vmem],
+        in_specs=[smem, smem, hbm, hbm, hbm, hbm],
         out_specs=(vmem,) * 4,
         scratch_shapes=[
+            pltpu.VMEM((CH, VOX), BF16),
+            pltpu.VMEM((CH, VOX), BF16),
+            pltpu.VMEM((CH, 27 * CH), BF16),
+            pltpu.VMEM((CH, 27 * CH), BF16),
+            dma((4,)),
             pltpu.VMEM((E + 2, E + 2, E, 256), F32),
             pltpu.VMEM((E + 2, E + 2, E, 256), F32),
             pltpu.VMEM((E + 2, E + 2, E, 256), F32),
@@ -488,7 +509,10 @@
         out_shape=(brick, brick, grad, grad),
         in_specs=[vmem] * 4,
         out_specs=(vmem,) * 4,
-    )(output, input_grad, first_sum, second_sum)
+    )(*(
+        pltpu.with_memory_space_constraint(value, pltpu.VMEM)
+        for value in (output, input_grad, first_sum, second_sum)
+    ))
     return (output[None, None, None], input_grad[None, None, None], first_grad, second_grad)
 
 

time: 37.9 us -> 35.1 us (0.926)
  Pallas kernels: 35.8 us -> 33 us
    pallas_call x1, Pallas kernels: 33.7 us -> 32 us  [body(): pl.pallas_call(functools.partial(kernel, n_gz, n_gy), out_shape=(pltpu.VM...]
    pallas_call x1, Pallas kernels: 2.09 us -> 0.99 us  [body(): pl.pallas_call(functools.partial(finish, scale), out_shape=(brick, brick,...]
where the time goes in v3:
time: 35.1 us; the launch traced here: 34.9 us
  Pallas kernels  33 us (94%)
  between operations  1.93 us (5%)
    pallas_call x1, Pallas kernels, body(): pl.pallas_call(functools.partial(kernel, n_gz, n_gy), out_shape=(pltpu.VM...  32 us
    pallas_call x1, Pallas kernels, body(): pl.pallas_call(functools.partial(finish, scale), out_shape=(brick, brick,...  0.99 us

profile of v3, /device:TPU:0, one launch (start us, length us, event | category | flops | bytes accessed | tf_op | source)
XLA Modules:
  0.0 34.9 jit_solution(17036339369073994168)
XLA Ops:
  1.9 32.0 %shard_map.93 = (bf16[64,512]{1,0:T(8,128)(2,1)S(1)}, bf16[64,512]{1,0:T(8,128)(2,1)S(1)}, bf16[64,1728]{1,0:T(8,128)(2,1)S(1)}, bf16[64,1728]{1,0:T(8,128)(2,1)S(1)}) custom-call(s32[1]{0:T(128)} %bitcast.6.place_ref, s32[1]{0:T(128)} %bitcast.7.count_ref, bf16[64,512]{1,0:T(8,128)(2,1)} %bitcast.8, bf16[64,512]{1,0:T(8,128)(2,1)} %bitcast.9, ...), custom_call_target="tpu_custom_call" | custom-call | tf_op jit(solution)/shard_map/pallas_call | solution.py:459
  33.9 1.0 %shard_map.94 = (bf16[64,512]{1,0:T(8,128)(2,1)}, bf16[64,512]{1,0:T(8,128)(2,1)}, f32[64,1728]{1,0:T(8,128)}, f32[64,1728]{1,0:T(8,128)}) custom-call(bf16[64,512]{1,0:T(8,128)(2,1)S(1)} %get-tuple-element.12.out_in, bf16[64,512]{1,0:T(8,128)(2,1)S(1)} %get-tuple-element.13.gin_in, bf16[64,1728]{1,0:T(8,128)(2,1)S(1)} %get-tuple-element.14.g1_in, ...), custom_call_target="tpu_custom_call" | custom-call | tf_op jit(solution)/shard_map/pallas_call | solution.py:507
